TPU v7x, 128 devices: a whole 4x4x4 slice. The times are simulated.
128 devices in a mesh: frag: 4 (over y_hi, core), aux: 16 (over z, x), orb: 2 (over y_lo).
Axes of the slice: x: 4, y: 4 (y_hi: 2, y_lo: 2; y = y_hi * 2 + y_lo), z: 4, core: 2. Of those that a mesh axis runs over, the one named last changes fastest.
Arguments:
- density: bfloat16 [16384, 2, 8192], P('frag', 'orb', 'aux'), may hold values from -0.046875 to 0.046875
- bath: bfloat16 [16, 2, 8192, 128], P('frag', 'orb', 'aux'), may hold values from -1 to 1
- factor: bfloat16 [16384, 16384], P('orb', 'aux'), may hold values from -6 to 6
- frag_index: int32 [16, 128], replicated, may hold values from 0 to 16383, as said below
- nfrag: int32 [16], replicated, may hold values from 1 to 128
- nbath: int32 [16], replicated, may hold values from 1 to 128
Outputs:
- projected: bfloat16 [16, 256, 16384], P('frag', 'orb', 'aux')
Inputs may be any that keep to these rules, and one draw needn't show every extreme that they name: `frag_index`: the 128 entries of one fragment's row are distinct basis functions; entries at or past nfrag are not read.
All inputs are finite; a program needn't handle non-finite values.
Results may differ from a plain program's by a relative error of at most 0.0049.
Values may be sent and summed in bfloat16 or wider, within the bound.
A program may use at most 128 MiB of HBM per device.

v0:
```python
import jax
import jax.numpy as jnp
from jax import lax
from jax.sharding import PartitionSpec as P


def per_device(density, bath, factor, frag_index, nfrag, nbath):
    local_rows = density.shape[0]
    block_cols = density.shape[2]
    density_local = density.reshape(local_rows, block_cols)
    group_size = bath.shape[0]
    frag_max = frag_index.shape[1]
    bath_max = bath.shape[3]
    frag_count = frag_index.shape[0]
    row_offset = lax.axis_index("frag") * local_rows
    local_index = frag_index - row_offset
    owned_rows = (local_index >= 0) & (local_index < local_rows)
    picked = jnp.take(density_local, jnp.clip(local_index, 0, local_rows - 1).reshape(-1), axis=0)
    picked = picked.reshape(frag_count, frag_max, block_cols)
    picked = jnp.where(owned_rows[:, :, None], picked, jnp.zeros_like(picked))
    gathered_rows = (
        lax.psum_scatter(picked, "frag", scatter_dimension=0, tiled=True)
        .astype(jnp.float32)
        .astype(jnp.bfloat16)
    )
    first_frag = lax.axis_index("frag") * group_size
    my_nfrag = lax.dynamic_slice_in_dim(nfrag, first_frag, group_size)
    my_nbath = lax.dynamic_slice_in_dim(nbath, first_frag, group_size)
    frag_live = jnp.arange(frag_max, dtype=jnp.int32)[None, :] < my_nfrag[:, None]
    bath_live = jnp.arange(bath_max, dtype=jnp.int32)[None, :] < my_nbath[:, None]
    gathered_rows = jnp.where(frag_live[:, :, None], gathered_rows, jnp.zeros_like(gathered_rows))
    bath_cols = bath.reshape(group_size, block_cols, bath_max)
    bath_cols = jnp.where(bath_live[:, None, :], bath_cols, jnp.zeros_like(bath_cols))
    initial = jnp.concatenate([jnp.swapaxes(gathered_rows, 1, 2), bath_cols], axis=2)
    live_cols = jnp.concatenate([frag_live, bath_live], axis=1).astype(jnp.float32)
    kmax_cols = initial.shape[2]
    identity_pad = jnp.eye(kmax_cols, dtype=jnp.float32)[None] * (1.0 - live_cols)[:, :, None]
    gram_part = jnp.einsum("fmk,fml->fkl", initial, initial, preferred_element_type=jnp.float32)
    gram_total = lax.psum(gram_part, ("aux", "orb")) + identity_pad
    cholesky_low = jnp.linalg.cholesky(gram_total)
    coeffs = lax.linalg.triangular_solve(
        cholesky_low, initial.astype(jnp.float32), left_side=False, lower=True, transpose_a=True
    )
    coeffs = coeffs.astype(jnp.bfloat16)
    partial_value = jnp.einsum(
        "fmk,mq->fkq",
        lax.all_gather(coeffs, "aux", axis=1, tiled=True),
        factor,
        preferred_element_type=jnp.float32,
    )
    summed = lax.psum_scatter(partial_value, "orb", scatter_dimension=1, tiled=True)
    return summed.astype(jnp.bfloat16)


def solution(mesh):
    placed = (
        P("frag", "orb", "aux"),
        P("frag", "orb", "aux", None),
        P("orb", "aux"),
        P(),
        P(),
        P(),
    )
    return jax.shard_map(
        per_device, mesh=mesh, in_specs=placed, out_specs=P("frag", "orb", "aux"), check_vma=False
    )
```

profile of v0, /device:TPU:1, one launch (start us, length us, event | category | flops | bytes accessed | tf_op | source)
XLA Modules:
  0.0 812.8 jit_solution(12678690382864565310)
XLA Ops:
  6.5 0.7 compare_and_fusion
  7.3 10.3 %gather_fusion = bf16[2048,512]{1,0:T(8,128)(2,1)S(1)} fusion(bf16[4096,512]{1,0:T(8,128)(2,1)} %bitcast.50, s32[2048]{0:T(1024)S(1)} %broadcast_clamp_fusion), kind=kCustom, calls=%fused_computation | custom fusion | bytes 4202496 | tf_op jit(solution)/shard_map/jit(_take)/gather | solution.py:18
  17.6 2.4 copy.24
  20.0 3.2 select_select_fusion
  23.2 0.0 reduce-scatter.3.cloned.1.call-update
  23.2 0.0 all-reduce.3.cloned.1.call-start
  23.3 0.6 copy-done.5
  23.8 0.1 dynamic_slice.6
  23.9 0.1 dynamic_slice.7
  24.0 0.1 iota_compare_fusion.4
  24.1 0.2 copy-done.4
  24.3 40.2 %reduce-scatter.3.cloned.1.call-done = bf16[4,128,512]{1,2,0:T(8,128)(2,1)} async-done(((bf16[16,128,512]{1,2,0:T(8,128)(2,1)}), bf16[4,128,512]{1,2,0:T(8,128)(2,1)}) %reduce-scatter.3.cloned.1.call-update) | async-done | bytes 524304 | tf_op jit(solution)/shard_map/reduce_scatter | solution.py:22
  64.5 1.1 fusion.8
  65.6 1.5 fusion.2
  67.1 0.0 all-reduce.3.cloned.1.call-update
  67.1 0.2 all-gather.2.cloned.1.call-start
  67.5 286.9 %all-reduce.3.cloned.1.call-done = f32[4,256,256]{1,2,0:T(8,128)} async-done(((f32[4,256,256]{1,2,0:T(8,128)}), f32[4,256,256]{1,2,0:T(8,128)}) %all-reduce.3.cloned.1.call-update) | async-done | bytes 1048592 | tf_op jit(solution)/shard_map/psum | solution.py:39
  354.4 1.4 multiply_add_fusion
  355.9 0.3 copy.27
  356.2 0.2 fusion.6
  356.4 46.9 %custom-call.16 = f32[4,128,128]{2,1,0:T(8,128)S(1)} custom-call(f32[4,128,128]{2,1,0:T(8,128)S(1)} %cholesky.122), custom_call_target="Cholesky" | custom-call | tf_op jit(solution)/shard_map/jit(cholesky)/cholesky | solution.py:40
  403.3 39.3 %custom-call.17 = f32[4,1,128,128]{2,3,1,0:T(8,128)S(1)} custom-call(f32[4,1,128,128]{3,2,1,0:T(8,128)S(1)} %select_bitcast_fusion), custom_call_target="InvertDiagBlocksLowerTriangular" | custom-call | tf_op jit(solution)/shard_map/jit(cholesky)/cholesky | solution.py:40
  442.6 0.1 cholesky.117
  442.7 0.4 constant_dynamic-update-slice_fusion.1
  443.1 0.7 convolution_subtract_fusion.1
  443.8 46.9 %custom-call.18 = f32[4,128,128]{2,1,0:T(8,128)S(1)} custom-call(f32[4,128,128]{2,1,0:T(8,128)S(1)} %convolution_subtract_fusion.1), custom_call_target="Cholesky" | custom-call | tf_op jit(solution)/shard_map/jit(cholesky)/cholesky | solution.py:40
  490.7 0.1 select_reduce_fusion
  490.8 0.1 compare_reduce_fusion
  490.9 0.1 compare_reduce_fusion.1
  491.0 0.2 select_select_fusion.1
  491.2 0.1 triangular_solve.63
  491.3 5.4 while.1
  491.3 0.6 fusion.25
  491.9 2.1 bitcast_dynamic-update-slice_fusion.2
  494.0 0.6 fusion.25
  494.6 2.1 bitcast_dynamic-update-slice_fusion.2
  496.7 79.4 %custom-call.19 = f32[4,2,128,128]{2,3,1,0:T(8,128)S(1)} custom-call(f32[4,2,128,128]{3,2,1,0:T(8,128)} %bitcast.54), custom_call_target="InvertDiagBlocksLowerTriangular" | custom-call | tf_op jit(solution)/shard_map/triangular_solve | solution.py:41
  576.1 0.6 fusion.18
  576.8 1.8 convolution_subtract_fusion
  578.6 1.1 convolution_convert_fusion
  579.7 1.0 pad_maximum_fusion
  580.7 0.0 all-gather.2.cloned.1.call-update
  580.7 0.0 reduce-scatter.5.cloned.1.call-start
  580.8 141.7 %all-gather.2.cloned.1.call-done = bf16[4,8192,256]{1,2,0:T(8,128)(2,1)} async-done(((bf16[4,512,256]{1,2,0:T(8,128)(2,1)}), bf16[4,8192,256]{1,2,0:T(8,128)(2,1)}) %all-gather.2.cloned.1.call-update) | async-done | bytes 16777232 | tf_op jit(solution)/shard_map/all_gather | solution.py:47
  722.5 23.5 %fusion = f32[4,256,1024]{2,1,0:T(8,128)} fusion(bf16[4,8192,256]{1,2,0:T(8,128)(2,1)} %all-gather.2.cloned.1.call-done, bf16[8192,1024]{1,0:T(8,128)(2,1)} %param.8), kind=kOutput, calls=%fused_computation.3 | convolution fusion | flops 17179869184 | bytes 37748736 | tf_op jit(solution)/shard_map/fmk,mq->fkq/dot_general | solution.py:45
  746.0 0.0 reduce-scatter.5.cloned.1.call-update
  746.0 57.5 %reduce-scatter.5.cloned.1.call-done = f32[4,128,1024]{2,1,0:T(8,128)} async-done(((f32[4,256,1024]{2,1,0:T(8,128)}), f32[4,128,1024]{2,1,0:T(8,128)}) %reduce-scatter.5.cloned.1.call-update) | async-done | bytes 2097168 | tf_op jit(solution)/shard_map/reduce_scatter | solution.py:51
  803.5 2.7 convert_element_type.23
  (28 shorter events, 0.2 us)
Async XLA Ops:
  6.5 58.0 %reduce-scatter.3.cloned.1.call-start = ((), (), s32[]{:S(2)}) async-start(), calls=%async_computation.2 | async-start | bytes 2621440 | tf_op jit(solution)/shard_map/reduce_scatter | solution.py:22
  23.2 0.7 copy-start.5
  23.2 0.7 copy-start.6
  23.2 1.1 copy-start.4
  23.2 331.2 %all-reduce.3.cloned.1.call-start = ((), (), s32[]{:S(2)}) async-start(), calls=%async_computation.3 | async-start | bytes 2097152 | tf_op jit(solution)/shard_map/psum | solution.py:39
  24.3 42.8 %copy-start.2 = (bf16[4,512,128]{2,1,0:T(8,128)(2,1)}, bf16[4,512,128]{2,1,0:T(8,128)(2,1)S(1)}, u32[]{:S(2)}) copy-start(bf16[4,512,128]{2,1,0:T(8,128)(2,1)S(1)} %bitcast_select_fusion) | copy-start | bytes 1572868
  67.1 655.4 %all-gather.2.cloned.1.call-start = ((), (), s32[]{:S(2)}) async-start(), calls=%async_computation.4 | async-start | bytes 17825792 | tf_op jit(solution)/shard_map/all_gather | solution.py:47
  354.4 1.8 copy-start
  491.0 85.1 %copy-start.1 = (bf16[4,128,512]{1,2,0:T(8,128)(2,1)S(1)}, bf16[4,128,512]{1,2,0:T(8,128)(2,1)}, u32[]{:S(2)}) copy-start(bf16[4,128,512]{1,2,0:T(8,128)(2,1)} %reduce-scatter.3.cloned.1.call-done) | copy-start | bytes 1572868
  491.3 85.5 %copy-start.3 = (bf16[4,512,128]{2,1,0:T(8,128)(2,1)S(1)}, bf16[4,512,128]{2,1,0:T(8,128)(2,1)}, u32[]{:S(2)}) copy-start(bf16[4,512,128]{2,1,0:T(8,128)(2,1)} %copy-done.2) | copy-start | bytes 1572868
  580.7 222.8 %reduce-scatter.5.cloned.1.call-start = ((), (), s32[]{:S(2)}) async-start(), calls=%async_computation.5 | async-start | bytes 6291456 | tf_op jit(solution)/shard_map/reduce_scatter | solution.py:51
Sparse Core Ops, SparseCore 0:
  23.3 41.1 reduce-scatter.2
  67.2 287.1 all-reduce.2
  580.9 141.6 all-gather.1
  746.2 57.3 reduce-scatter.4
where the time goes:
time: 813 us
  waiting for transfers between devices  526 us (65%)
  other arithmetic  224 us (28%)
  matrix products  29.6 us (4%)
  local copies, waits for them, and re-layouts  19.5 us (2%)
  between operations  13.4 us (2%)
    psum x1, waiting for transfers between devices, per_device(): gram_total = lax.psum(gram_part, ('aux', 'orb')) + identity_pad  287 us
    all_gather x1, waiting for transfers between devices, per_device(): lax.all_gather(coeffs, 'aux', axis=1, tiled=True)  142 us
    another operation x10, other arithmetic, per_device(): cholesky_low = jnp.linalg.cholesky(gram_total)  133 us
    another operation x5, other arithmetic, per_device(): lax.linalg.triangular_solve(cholesky_low, initial.astype(jnp.float32), le...  80.7 us
    reduce_scatter x1, waiting for transfers between devices, per_device(): lax.psum_scatter(partial_value, 'orb', scatter_dimension=1, tiled=True)  57.5 us
    reduce_scatter x1, waiting for transfers between devices, per_device(): lax.psum_scatter(picked, 'frag', scatter_dimension=0, tiled=True)  40.2 us
    dot_general x1, matrix products, per_device(): jnp.einsum('fmk,mq->fkq', lax.all_gather(coeffs, 'aux', axis=1, tiled=Tru...  23.5 us
  transfers between devices with their start and end apart: 4, of which 4 were waited for; matrix products, arithmetic and copies ran while one was open for 0% of the time, Pallas kernels for 0%

commit v1 on v0

--- a/solution.py
+++ b/solution.py
@@ -36,7 +36,7 @@
     kmax_cols = initial.shape[2]
     identity_pad = jnp.eye(kmax_cols, dtype=jnp.float32)[None] * (1.0 - live_cols)[:, :, None]
     gram_part = jnp.einsum("fmk,fml->fkl", initial, initial, preferred_element_type=jnp.float32)
-    gram_total = lax.psum(gram_part, ("aux", "orb")) + identity_pad
+    gram_total = jnp.sum(lax.all_gather(gram_part, ("aux", "orb")), axis=0) + identity_pad
     cholesky_low = jnp.linalg.cholesky(gram_total)
     coeffs = lax.linalg.triangular_solve(
         cholesky_low, initial.astype(jnp.float32), left_side=False, lower=True, transpose_a=True

time: 813 us -> 1230 us (1.51)
  waiting for transfers between devices: 526 us -> 933 us
    all_gather x0 -> x1, waiting for transfers between devices: none -> 707 us  [per_device(): lax.all_gather(gram_part, ('aux', 'orb'))]
    psum x1 -> x0, waiting for transfers between devices: 287 us -> none  [per_device(): gram_total = lax.psum(gram_part, ('aux', 'orb')) + identity_pad]
    all_gather x1, waiting for transfers between devices: 142 us -> 128 us  [per_device(): lax.all_gather(coeffs, 'aux', axis=1, tiled=True)]
where the time goes in v1:
time: 1230 us
  waiting for transfers between devices  933 us (76%)
  other arithmetic  236 us (19%)
  matrix products  29.6 us (2%)
  local copies, waits for them, and re-layouts  19.7 us (2%)
  between operations  13.4 us (1%)
    all_gather x1, waiting for transfers between devices, per_device(): lax.all_gather(gram_part, ('aux', 'orb'))  707 us
    another operation x10, other arithmetic, per_device(): cholesky_low = jnp.linalg.cholesky(gram_total)  133 us
    all_gather x1, waiting for transfers between devices, per_device(): lax.all_gather(coeffs, 'aux', axis=1, tiled=True)  128 us
    another operation x5, other arithmetic, per_device(): lax.linalg.triangular_solve(cholesky_low, initial.astype(jnp.float32), le...  80.7 us
    reduce_scatter x1, waiting for transfers between devices, per_device(): lax.psum_scatter(partial_value, 'orb', scatter_dimension=1, tiled=True)  57.5 us
    reduce_scatter x1, waiting for transfers between devices, per_device(): lax.psum_scatter(picked, 'frag', scatter_dimension=0, tiled=True)  40.2 us
  transfers between devices with their start and end apart: 4, of which 4 were waited for; matrix products, arithmetic and copies ran while one was open for 0% of the time, Pallas kernels for 0%

profile of v1, /device:TPU:1, one launch (start us, length us, event | category | flops | bytes accessed | tf_op | source)
XLA Modules:
  0.0 1231.9 jit_solution(226728826755738780)
XLA Ops:
  6.5 0.7 compare_and_fusion
  7.3 10.3 gather_fusion
  17.6 2.4 copy.32
  20.0 3.2 select_select_fusion
  23.2 0.0 reduce-scatter.3.cloned.1.call-update
  23.2 0.0 all-gather.6.cloned.1.call-start
  23.3 0.6 copy-done.4
  23.8 0.1 dynamic_slice.6
  23.9 0.1 dynamic_slice.7
  24.0 0.1 iota_compare_fusion.5
  24.1 0.2 copy-done.3
  24.3 40.2 %reduce-scatter.3.cloned.1.call-done = bf16[4,128,512]{1,2,0:T(8,128)(2,1)} async-done(((bf16[16,128,512]{1,2,0:T(8,128)(2,1)}), bf16[4,128,512]{1,2,0:T(8,128)(2,1)}) %reduce-scatter.3.cloned.1.call-update) | async-done | bytes 524304 | tf_op jit(solution)/shard_map/reduce_scatter | solution.py:22
  64.5 1.1 fusion.9
  65.6 1.5 fusion.2
  67.1 0.0 all-gather.6.cloned.1.call-update
  67.1 0.0 all-gather.4.cloned.1.call-start
  67.3 0.7 fusion.15
  68.0 707.2 %all-gather.6.cloned.1.call-done = f32[128,256,256]{2,1,0:T(8,128)} async-done(((f32[4,256,256]{2,1,0:T(8,128)}), f32[128,256,256]{2,1,0:T(8,128)}) %all-gather.6.cloned.1.call-update) | async-done | bytes 33554448 | tf_op jit(solution)/shard_map/all_gather | solution.py:39
  775.2 12.1 reduce_sum.11
  787.4 0.3 copy.34
  787.7 1.2 fusion.7
  788.9 46.9 %custom-call.16 = f32[4,128,128]{2,1,0:T(8,128)S(1)} custom-call(f32[4,128,128]{2,1,0:T(8,128)S(1)} %cholesky.122), custom_call_target="Cholesky" | custom-call | tf_op jit(solution)/shard_map/jit(cholesky)/cholesky | solution.py:40
  835.8 0.1 cholesky.117
  836.0 39.3 %custom-call.17 = f32[4,1,128,128]{2,3,1,0:T(8,128)S(1)} custom-call(f32[4,1,128,128]{3,2,1,0:T(8,128)S(1)} %select_bitcast_fusion), custom_call_target="InvertDiagBlocksLowerTriangular" | custom-call | tf_op jit(solution)/shard_map/jit(cholesky)/cholesky | solution.py:40
  875.3 0.4 constant_dynamic-update-slice_fusion.1
  875.7 0.7 convolution_subtract_fusion.1
  876.4 46.9 %custom-call.18 = f32[4,128,128]{2,1,0:T(8,128)S(1)} custom-call(f32[4,128,128]{2,1,0:T(8,128)S(1)} %convolution_subtract_fusion.1), custom_call_target="Cholesky" | custom-call | tf_op jit(solution)/shard_map/jit(cholesky)/cholesky | solution.py:40
  923.3 0.1 select_reduce_fusion
  923.3 0.1 compare_reduce_fusion
  923.4 0.1 compare_reduce_fusion.1
  923.6 0.2 select_select_fusion.1
  923.8 0.1 triangular_solve.66
  923.8 5.6 while.1
  923.8 0.6 fusion.27
  924.4 2.2 bitcast_dynamic-update-slice_fusion.2
  926.6 0.6 fusion.27
  927.2 2.2 bitcast_dynamic-update-slice_fusion.2
  929.4 79.4 %custom-call.19 = f32[4,2,128,128]{2,3,1,0:T(8,128)S(1)} custom-call(f32[4,2,128,128]{3,2,1,0:T(8,128)} %bitcast.58), custom_call_target="InvertDiagBlocksLowerTriangular" | custom-call | tf_op jit(solution)/shard_map/triangular_solve | solution.py:41
  1008.8 0.6 fusion.20
  1009.5 1.8 convolution_subtract_fusion
  1011.3 1.1 convolution_convert_fusion
  1012.4 1.0 pad_maximum_fusion
  1013.5 0.0 reduce-scatter.5.cloned.1.call-start
  1013.5 128.1 %all-gather.4.cloned.1.call-done = bf16[4,8192,256]{1,2,0:T(8,128)(2,1)} async-done(((bf16[4,512,256]{1,2,0:T(8,128)(2,1)}), bf16[4,8192,256]{1,2,0:T(8,128)(2,1)}) %all-gather.4.cloned.1.call-update) | async-done | bytes 16777232 | tf_op jit(solution)/shard_map/all_gather | solution.py:47
  1141.6 23.5 %fusion = f32[4,256,1024]{2,1,0:T(8,128)} fusion(bf16[4,8192,256]{1,2,0:T(8,128)(2,1)} %all-gather.4.cloned.1.call-done, bf16[8192,1024]{1,0:T(8,128)(2,1)} %param.8), kind=kOutput, calls=%fused_computation.3 | convolution fusion | flops 17179869184 | bytes 37748736 | tf_op jit(solution)/shard_map/fmk,mq->fkq/dot_general | solution.py:45
  1165.1 0.0 reduce-scatter.5.cloned.1.call-update
  1165.2 57.5 %reduce-scatter.5.cloned.1.call-done = f32[4,128,1024]{2,1,0:T(8,128)} async-done(((f32[4,256,1024]{2,1,0:T(8,128)}), f32[4,128,1024]{2,1,0:T(8,128)}) %reduce-scatter.5.cloned.1.call-update) | async-done | bytes 2097168 | tf_op jit(solution)/shard_map/reduce_scatter | solution.py:51
  1222.7 2.7 convert_element_type.27
  (26 shorter events, 0.2 us)
Async XLA Ops:
  6.5 58.0 %reduce-scatter.3.cloned.1.call-start = ((), (), s32[]{:S(2)}) async-start(), calls=%async_computation.2 | async-start | bytes 2621440 | tf_op jit(solution)/shard_map/reduce_scatter | solution.py:22
  23.2 0.7 copy-start.4
  23.2 0.7 copy-start.5
  23.2 1.1 copy-start.3
  23.2 752.0 %all-gather.6.cloned.1.call-start = ((), (), s32[]{:S(2)}) async-start(), calls=%async_computation.5 | async-start | bytes 34603008 | tf_op jit(solution)/shard_map/all_gather | solution.py:39
  24.3 42.8 %copy-start.1 = (bf16[4,512,128]{2,1,0:T(8,128)(2,1)}, bf16[4,512,128]{2,1,0:T(8,128)(2,1)S(1)}, u32[]{:S(2)}) copy-start(bf16[4,512,128]{2,1,0:T(8,128)(2,1)S(1)} %bitcast_select_fusion) | copy-start | bytes 1572868
  67.1 1074.5 %all-gather.4.cloned.1.call-start = ((), (), s32[]{:S(2)}) async-start(), calls=%async_computation.3 | async-start | bytes 17825792 | tf_op jit(solution)/shard_map/all_gather | solution.py:47
  923.6 85.3 %copy-start = (bf16[4,128,512]{1,2,0:T(8,128)(2,1)S(1)}, bf16[4,128,512]{1,2,0:T(8,128)(2,1)}, u32[]{:S(2)}) copy-start(bf16[4,128,512]{1,2,0:T(8,128)(2,1)} %reduce-scatter.3.cloned.1.call-done) | copy-start | bytes 1572868
  923.8 85.6 %copy-start.2 = (bf16[4,512,128]{2,1,0:T(8,128)(2,1)S(1)}, bf16[4,512,128]{2,1,0:T(8,128)(2,1)}, u32[]{:S(2)}) copy-start(bf16[4,512,128]{2,1,0:T(8,128)(2,1)} %copy-done.1) | copy-start | bytes 1572868
  1013.5 209.2 %reduce-scatter.5.cloned.1.call-start = ((), (), s32[]{:S(2)}) async-start(), calls=%async_computation.4 | async-start | bytes 6291456 | tf_op jit(solution)/shard_map/reduce_scatter | solution.py:51
Sparse Core Ops, SparseCore 0:
  23.3 41.1 reduce-scatter.2
  67.2 707.9 all-gather.5
  1013.6 128.0 all-gather.3
  1165.3 57.3 reduce-scatter.4
